TPU v7x, 256 devices: a whole 4x4x8 slice. The times are simulated.
256 devices in a mesh: lat: 8 (over z), lon: 32 (over x, y, core).
Axes of the slice: x: 4, y: 4, z: 8, core: 2. Of those that a mesh axis runs over, the one named last changes fastest.
Arguments:
- inputs: bfloat16 [4, 128, 256, 1024], P(None, 'lat', 'lon'), may hold values from -6 to 6
- w_reduce: bfloat16 [1024, 256], replicated, may hold values from -0.1875 to 0.1875
- gain_reduce: float32 [256], replicated, may hold values from 0.1 to 1.9
- bias_reduce: float32 [256], replicated, may hold values from -3 to 3
- w_dilated: bfloat16 [3, 3, 256, 256], replicated, may hold values from -0.125 to 0.125
- gain_dilated: float32 [256], replicated, may hold values from 0.1 to 1.9
- bias_dilated: float32 [256], replicated, may hold values from -3 to 3
- w_expand: bfloat16 [256, 1024], replicated, may hold values from -0.375 to 0.375
- gain_expand: float32 [1024], replicated, may hold values from 0.1 to 1.9
- bias_expand: float32 [1024], replicated, may hold values from -3 to 3
- grad_out: bfloat16 [4, 128, 256, 1024], P(None, 'lat', 'lon'), may hold values from -6 to 6
- labels: int32 [4, 128, 256], P(None, 'lat', 'lon'), may hold values from 0 to 2
- class_weight: float32 [3], replicated, may hold values from 0.5 to 8
Outputs:
- grad_inputs: bfloat16 [4, 128, 256, 1024], P(None, 'lat', 'lon')
- grad_reduce: bfloat16 [1024, 256], replicated
- grad_dilated: bfloat16 [3, 3, 256, 256], replicated
- grad_expand: bfloat16 [256, 1024], replicated
All inputs are finite; a program needn't handle non-finite values.
Results may differ from a plain program's by a relative error of at most 0.0079.
Values may be sent and summed in bfloat16 or wider, within the bound.
A program may use at most 64 MiB of HBM per device.

v0:
```python
import jax
import jax.numpy as jnp
from jax import lax
from jax.sharding import PartitionSpec as P


def with_halo(cells, sides, width, closed):
    for axis, dim in sides:
        count = lax.axis_size(axis)
        ends = count if closed else count - 1
        head = lax.slice_in_dim(cells, 0, width, axis=dim)
        tail = lax.slice_in_dim(cells, cells.shape[dim] - width, cells.shape[dim], axis=dim)
        cells = jnp.concatenate(
            [
                lax.ppermute(tail, axis, [(i, (i + 1) % count) for i in range(ends)]),
                cells,
                lax.ppermute(head, axis, [((i + 1) % count, i) for i in range(ends)]),
            ],
            axis=dim,
        )
    return cells


def smooth(pre):
    return pre * jax.nn.sigmoid(pre)


def slope(pre):
    sig = jax.nn.sigmoid(pre)
    return sig * (1.0 + pre * (1.0 - sig))


def gather_taps(padded, height, width, flipped):
    pieces = []
    for row_tap in range(3):
        for col_tap in range(3):
            off_row = 4 - 2 * row_tap if flipped else 2 * row_tap
            off_col = 4 - 2 * col_tap if flipped else 2 * col_tap
            pieces.append(padded[:, off_row : off_row + height, off_col : off_col + width, :])
    stacked = jnp.concatenate(pieces, axis=-1)
    return stacked.reshape(-1, stacked.shape[-1])


def pixel_sum(left, right):
    return lax.dot_general(
        left, right, (((0,), (0,)), ((), ())), preferred_element_type=jnp.float32
    )


def per_device(
    inputs,
    w_reduce,
    gain_reduce,
    bias_reduce,
    w_dilated,
    gain_dilated,
    bias_dilated,
    w_expand,
    gain_expand,
    bias_expand,
    grad_out,
    labels,
    class_weight,
):
    batch, height, width, chan_in = inputs.shape
    chan_mid = w_reduce.shape[1]
    pixels = batch * height * width
    kernel = w_dilated.reshape(9 * chan_mid, chan_mid)
    kernel_back = jnp.transpose(w_dilated, (0, 1, 3, 2)).reshape(9 * chan_mid, chan_mid)
    classes = jnp.arange(class_weight.shape[0], dtype=jnp.int32)
    flat_in = inputs.reshape(pixels, chan_in)
    pre_one = (
        jnp.dot(flat_in, w_reduce, preferred_element_type=jnp.float32) * gain_reduce + bias_reduce
    )
    mid_one = smooth(pre_one).astype(jnp.bfloat16).reshape(batch, height, width, chan_mid)
    rows_one = with_halo(mid_one, (("lat", 1),), 2, False)
    padded_one = with_halo(rows_one, (("lon", 2),), 2, True)
    taps_one = gather_taps(padded_one, height, width, False)
    pre_two = (
        jnp.dot(taps_one, kernel, preferred_element_type=jnp.float32) * gain_dilated + bias_dilated
    )
    mid_two = smooth(pre_two).astype(jnp.bfloat16)
    pre_three = (
        jnp.dot(mid_two, w_expand, preferred_element_type=jnp.float32) * gain_expand
        + bias_expand
        + flat_in.astype(jnp.float32)
    )
    pixel_weight = jnp.sum(
        jnp.where(labels.reshape(pixels, 1) == classes, class_weight, 0.0), axis=-1
    )
    grad_full = (
        grad_out.reshape(pixels, chan_in).astype(jnp.float32)
        * pixel_weight[:, None]
        * slope(pre_three)
    )
    grad_three = (grad_full * gain_expand).astype(jnp.bfloat16)
    term_expand = pixel_sum(mid_two, grad_three)
    grad_two = (
        jnp.dot(grad_three, w_expand.T, preferred_element_type=jnp.float32)
        * slope(pre_two)
        * gain_dilated
    ).astype(jnp.bfloat16)
    term_dilated = pixel_sum(taps_one, grad_two)
    rows_two = with_halo(grad_two.reshape(batch, height, width, chan_mid), (("lat", 1),), 2, False)
    padded_two = with_halo(rows_two, (("lon", 2),), 2, True)
    taps_two = gather_taps(padded_two, height, width, True)
    grad_one = (
        jnp.dot(taps_two, kernel_back, preferred_element_type=jnp.float32)
        * slope(pre_one)
        * gain_reduce
    ).astype(jnp.bfloat16)
    term_reduce = pixel_sum(flat_in, grad_one)
    grad_inputs = (
        jnp.dot(grad_one, w_reduce.T, preferred_element_type=jnp.float32) + grad_full
    ).astype(jnp.bfloat16)
    total_reduce, total_dilated, total_expand = lax.psum(
        (term_reduce, term_dilated, term_expand), ("lat", "lon")
    )
    grad_reduce = total_reduce.astype(jnp.bfloat16)
    grad_dilated = total_dilated.astype(jnp.bfloat16)
    grad_expand = total_expand.astype(jnp.bfloat16)
    grad_dilated = grad_dilated.reshape(3, 3, chan_mid, chan_mid)
    return (
        grad_inputs.reshape(batch, height, width, chan_in),
        grad_reduce,
        grad_dilated,
        grad_expand,
    )


def solution(mesh):
    return jax.shard_map(
        per_device,
        mesh=mesh,
        in_specs=(
            P(None, "lat", "lon", None),
            P(),
            P(),
            P(),
            P(),
            P(),
            P(),
            P(),
            P(),
            P(),
            P(None, "lat", "lon", None),
            P(None, "lat", "lon"),
            P(),
        ),
        out_specs=(P(None, "lat", "lon", None), P(), P(), P()),
        check_vma=False,
    )
```

profile of v0, /device:TPU:64, one launch (start us, length us, event | category | flops | bytes accessed | tf_op | source)
XLA Modules:
  0.0 187.6 jit_solution(14700682848667514248)
XLA Ops:
  0.6 1.0 copy-done
  1.7 1.8 multiply_convert_fusion.2
  3.5 3.8 %collective-permute-start = (bf16[4,2,8,256]{3,2,1,0:T(8,128)(2,1)S(1)}, bf16[4,2,8,256]{3,2,1,0:T(8,128)(2,1)S(1)}, u32[]{:S(2)}, u32[]{:S(2)}) collective-permute-start(bf16[4,2,8,256]{3,2,1,0:T(8,128)(2,1)S(1)} %get-tuple-element.45), channel_id=1, source_target_pairs={{0,32},{32,64},{64,96},{96,128},{128,160},{160,192},{192,224},{1,3... | collective-permute-start | bytes 98312 | tf_op jit(solution)/shard_map/ppermute | solution.py:15
  7.3 2.0 %collective-permute-start.1 = (bf16[4,2,8,256]{3,2,1,0:T(8,128)(2,1)S(1)}, bf16[4,2,8,256]{3,2,1,0:T(8,128)(2,1)S(1)}, u32[]{:S(2)}, u32[]{:S(2)}) collective-permute-start(bf16[4,2,8,256]{3,2,1,0:T(8,128)(2,1)S(1)} %get-tuple-element.46), channel_id=1, source_target_pairs={{32,0},{64,32},{96,64},{128,96},{160,128},{192,160},{224,192},{33,... | collective-permute-start | bytes 98312 | tf_op jit(solution)/shard_map/ppermute | solution.py:17
  9.6 1.5 copy.22
  11.2 3.1 %collective-permute-done.1 = bf16[4,2,8,256]{3,2,1,0:T(8,128)(2,1)S(1)} collective-permute-done((bf16[4,2,8,256]{3,2,1,0:T(8,128)(2,1)S(1)}, bf16[4,2,8,256]{3,2,1,0:T(8,128)(2,1)S(1)}, u32[]{:S(2)}, u32[]{:S(2)}) %collective-permute-start.1) | collective-permute-done | bytes 32800 | tf_op jit(solution)/shard_map/ppermute | solution.py:17
  14.5 5.1 %collective-permute-start.3 = (bf16[4,20,2,256]{3,2,1,0:T(2,128)(2,1)S(1)}, bf16[4,20,2,256]{3,2,1,0:T(2,128)(2,1)S(1)}, u32[]{:S(2)}, u32[]{:S(2)}) collective-permute-start(bf16[4,20,2,256]{3,2,1,0:T(2,128)(2,1)S(1)} %get-tuple-element.37), channel_id=1, source_target_pairs={{1,0},{2,1},{3,2},{4,3},{5,4},{6,5},{7,6},{8,7},{9,8},{10,9},{11,1... | collective-permute-start | bytes 245768 | tf_op jit(solution)/shard_map/ppermute | solution.py:17
  19.6 2.1 %collective-permute-done.2 = bf16[4,20,2,256]{3,2,1,0:T(2,128)(2,1)S(1)} collective-permute-done((bf16[4,20,2,256]{3,2,1,0:T(2,128)(2,1)S(1)}, bf16[4,20,2,256]{3,2,1,0:T(2,128)(2,1)S(1)}, u32[]{:S(2)}, u32[]{:S(2)}) %collective-permute-start.2) | collective-permute-done | bytes 81952 | tf_op jit(solution)/shard_map/ppermute | solution.py:15
  22.9 0.8 fusion.2
  24.6 1.3 fusion
  26.4 0.8 fusion.14
  27.3 5.1 %collective-permute-start.4 = (bf16[4,2,8,256]{3,2,1,0:T(8,128)(2,1)S(1)}, bf16[4,2,8,256]{3,2,1,0:T(8,128)(2,1)S(1)}, u32[]{:S(2)}, u32[]{:S(2)}) collective-permute-start(bf16[4,2,8,256]{3,2,1,0:T(8,128)(2,1)S(1)} %get-tuple-element.41), channel_id=1, source_target_pairs={{0,32},{32,64},{64,96},{96,128},{128,160},{160,192},{192,224},{1,3... | collective-permute-start | bytes 98312 | tf_op jit(solution)/shard_map/ppermute | solution.py:15
  32.4 1.9 %collective-permute-start.5 = (bf16[4,2,8,256]{3,2,1,0:T(8,128)(2,1)S(1)}, bf16[4,2,8,256]{3,2,1,0:T(8,128)(2,1)S(1)}, u32[]{:S(2)}, u32[]{:S(2)}) collective-permute-start(bf16[4,2,8,256]{3,2,1,0:T(8,128)(2,1)S(1)} %get-tuple-element.42), channel_id=1, source_target_pairs={{32,0},{64,32},{96,64},{128,96},{160,128},{192,160},{224,192},{33,... | collective-permute-start | bytes 98312 | tf_op jit(solution)/shard_map/ppermute | solution.py:17
  34.3 1.5 fusion.7
  35.8 2.4 %collective-permute-done.5 = bf16[4,2,8,256]{3,2,1,0:T(8,128)(2,1)S(1)} collective-permute-done((bf16[4,2,8,256]{3,2,1,0:T(8,128)(2,1)S(1)}, bf16[4,2,8,256]{3,2,1,0:T(8,128)(2,1)S(1)}, u32[]{:S(2)}, u32[]{:S(2)}) %collective-permute-start.5) | collective-permute-done | bytes 32800 | tf_op jit(solution)/shard_map/ppermute | solution.py:17
  38.3 3.7 %collective-permute-start.6 = (bf16[4,20,2,256]{3,2,1,0:T(2,128)(2,1)S(1)}, bf16[4,20,2,256]{3,2,1,0:T(2,128)(2,1)S(1)}, u32[]{:S(2)}, u32[]{:S(2)}) collective-permute-start(bf16[4,20,2,256]{3,2,1,0:T(2,128)(2,1)S(1)} %get-tuple-element.34), channel_id=1, source_target_pairs={{1,0},{2,1},{3,2},{4,3},{5,4},{6,5},{7,6},{8,7},{9,8},{10,9},{11,1... | collective-permute-start | bytes 245768 | tf_op jit(solution)/shard_map/ppermute | solution.py:17
  42.1 2.0 %collective-permute-done.6 = bf16[4,20,2,256]{3,2,1,0:T(2,128)(2,1)S(1)} collective-permute-done((bf16[4,20,2,256]{3,2,1,0:T(2,128)(2,1)S(1)}, bf16[4,20,2,256]{3,2,1,0:T(2,128)(2,1)S(1)}, u32[]{:S(2)}, u32[]{:S(2)}) %collective-permute-start.6) | collective-permute-done | bytes 81952 | tf_op jit(solution)/shard_map/ppermute | solution.py:17
  44.1 5.1 %collective-permute-done.7 = bf16[4,20,2,256]{3,2,1,0:T(2,128)(2,1)S(1)} collective-permute-done((bf16[4,20,2,256]{3,2,1,0:T(2,128)(2,1)S(1)}, bf16[4,20,2,256]{3,2,1,0:T(2,128)(2,1)S(1)}, u32[]{:S(2)}, u32[]{:S(2)}) %collective-permute-start.7) | collective-permute-done | bytes 81952 | tf_op jit(solution)/shard_map/ppermute | solution.py:15
  50.1 1.0 copy-done.2
  51.1 0.8 fusion.5
  51.9 1.5 convolution_bitcast_fusion
  53.4 1.5 add_convert_fusion
  54.8 131.7 %all-reduce.2 = (bf16[1024,256]{0,1:T(8,128)(2,1)S(1)}, bf16[2304,256]{1,0:T(8,128)(2,1)}, bf16[256,1024]{1,0:T(8,128)(2,1)}) all-reduce(f32[1024,256]{0,1:T(8,128)} %convolution_bitcast_fusion, f32[2304,256]{1,0:T(8,128)S(1)} %fusion.14, f32[256,1024]{1,0:T(8,128)} %fusion.7), channel_id=1, replica_groups=mesh['lat'=8,'lon'=32] {'lat','lon'}, use_global_device_ids=true, to_apply=%region_1.2 | all-reduce | flops 1114112 | bytes 6684672 | tf_op jit(solution)/shard_map/psum | solution.py:116
  186.6 1.0 copy.23
  (62 shorter events, 4.0 us)
Async XLA Ops:
  0.6 1.0 copy-start
  1.7 7.7 %copy-start.4 = (s32[4,16,8]{1,2,0:T(8,128)S(1)}, s32[4,16,8]{1,2,0:T(8,128)}, u32[]{:S(2)}) copy-start(s32[4,16,8]{1,2,0:T(8,128)} %param.24) | copy-start | bytes 6148
  1.7 7.9 %copy-start.6 = (f32[3]{0:T(128)S(1)}, f32[3]{0:T(128)}, u32[]{:S(2)}) copy-start(f32[3]{0:T(128)} %param.25) | copy-start | bytes 40
  1.7 8.0 %copy-start.1 = (bf16[3,3,256,256]{3,2,1,0:T(8,128)(2,1)S(1)}, bf16[3,3,256,256]{3,2,1,0:T(8,128)(2,1)}, u32[]{:S(2)}) copy-start(bf16[3,3,256,256]{3,2,1,0:T(8,128)(2,1)} %param.17) | copy-start | bytes 3538948
  3.5 7.7 %collective-permute-start = (bf16[4,2,8,256]{3,2,1,0:T(8,128)(2,1)S(1)}, bf16[4,2,8,256]{3,2,1,0:T(8,128)(2,1)S(1)}, u32[]{:S(2)}, u32[]{:S(2)}) collective-permute-start(bf16[4,2,8,256]{3,2,1,0:T(8,128)(2,1)S(1)} %get-tuple-element.45), channel_id=1, source_target_pairs={{0,32},{32,64},{64,96},{96,128},{128,160},{160,192},{192,224},{1,3... | collective-permute-start | bytes 98312 | tf_op jit(solution)/shard_map/ppermute | solution.py:15
  7.3 6.9 %collective-permute-start.1 = (bf16[4,2,8,256]{3,2,1,0:T(8,128)(2,1)S(1)}, bf16[4,2,8,256]{3,2,1,0:T(8,128)(2,1)S(1)}, u32[]{:S(2)}, u32[]{:S(2)}) collective-permute-start(bf16[4,2,8,256]{3,2,1,0:T(8,128)(2,1)S(1)} %get-tuple-element.46), channel_id=1, source_target_pairs={{32,0},{64,32},{96,64},{128,96},{160,128},{192,160},{224,192},{33,... | collective-permute-start | bytes 98312 | tf_op jit(solution)/shard_map/ppermute | solution.py:17
  14.4 7.3 %collective-permute-start.2 = (bf16[4,20,2,256]{3,2,1,0:T(2,128)(2,1)S(1)}, bf16[4,20,2,256]{3,2,1,0:T(2,128)(2,1)S(1)}, u32[]{:S(2)}, u32[]{:S(2)}) collective-permute-start(bf16[4,20,2,256]{3,2,1,0:T(2,128)(2,1)S(1)} %get-tuple-element.38), channel_id=1, source_target_pairs={{0,1},{1,2},{2,3},{3,4},{4,5},{5,6},{6,7},{7,8},{8,9},{9,10},{10,1... | collective-permute-start | bytes 245768 | tf_op jit(solution)/shard_map/ppermute | solution.py:15
  14.5 7.2 %collective-permute-start.3 = (bf16[4,20,2,256]{3,2,1,0:T(2,128)(2,1)S(1)}, bf16[4,20,2,256]{3,2,1,0:T(2,128)(2,1)S(1)}, u32[]{:S(2)}, u32[]{:S(2)}) collective-permute-start(bf16[4,20,2,256]{3,2,1,0:T(2,128)(2,1)S(1)} %get-tuple-element.37), channel_id=1, source_target_pairs={{1,0},{2,1},{3,2},{4,3},{5,4},{6,5},{7,6},{8,7},{9,8},{10,9},{11,1... | collective-permute-start | bytes 245768 | tf_op jit(solution)/shard_map/ppermute | solution.py:17
  22.2 0.7 copy-start.10
  22.2 0.7 copy-start.11
  22.9 1.2 copy-start.3
  22.9 1.2 copy-start.5
  22.9 1.6 copy-start.7
  22.9 1.7 copy-start.8
  22.9 1.7 copy-start.9
  27.3 8.6 %collective-permute-start.4 = (bf16[4,2,8,256]{3,2,1,0:T(8,128)(2,1)S(1)}, bf16[4,2,8,256]{3,2,1,0:T(8,128)(2,1)S(1)}, u32[]{:S(2)}, u32[]{:S(2)}) collective-permute-start(bf16[4,2,8,256]{3,2,1,0:T(8,128)(2,1)S(1)} %get-tuple-element.41), channel_id=1, source_target_pairs={{0,32},{32,64},{64,96},{96,128},{128,160},{160,192},{192,224},{1,3... | collective-permute-start | bytes 98312 | tf_op jit(solution)/shard_map/ppermute | solution.py:15
  32.4 5.8 %collective-permute-start.5 = (bf16[4,2,8,256]{3,2,1,0:T(8,128)(2,1)S(1)}, bf16[4,2,8,256]{3,2,1,0:T(8,128)(2,1)S(1)}, u32[]{:S(2)}, u32[]{:S(2)}) collective-permute-start(bf16[4,2,8,256]{3,2,1,0:T(8,128)(2,1)S(1)} %get-tuple-element.42), channel_id=1, source_target_pairs={{32,0},{64,32},{96,64},{128,96},{160,128},{192,160},{224,192},{33,... | collective-permute-start | bytes 98312 | tf_op jit(solution)/shard_map/ppermute | solution.py:17
  38.3 5.8 %collective-permute-start.6 = (bf16[4,20,2,256]{3,2,1,0:T(2,128)(2,1)S(1)}, bf16[4,20,2,256]{3,2,1,0:T(2,128)(2,1)S(1)}, u32[]{:S(2)}, u32[]{:S(2)}) collective-permute-start(bf16[4,20,2,256]{3,2,1,0:T(2,128)(2,1)S(1)} %get-tuple-element.34), channel_id=1, source_target_pairs={{1,0},{2,1},{3,2},{4,3},{5,4},{6,5},{7,6},{8,7},{9,8},{10,9},{11,1... | collective-permute-start | bytes 245768 | tf_op jit(solution)/shard_map/ppermute | solution.py:17
  42.0 7.2 %collective-permute-start.7 = (bf16[4,20,2,256]{3,2,1,0:T(2,128)(2,1)S(1)}, bf16[4,20,2,256]{3,2,1,0:T(2,128)(2,1)S(1)}, u32[]{:S(2)}, u32[]{:S(2)}) collective-permute-start(bf16[4,20,2,256]{3,2,1,0:T(2,128)(2,1)S(1)} %get-tuple-element.33), channel_id=1, source_target_pairs={{0,1},{1,2},{2,3},{3,4},{4,5},{5,6},{6,7},{7,8},{8,9},{9,10},{10,1... | collective-permute-start | bytes 245768 | tf_op jit(solution)/shard_map/ppermute | solution.py:15
  49.8 1.3 copy-start.2
  49.9 1.3 copy-start.12
where the time goes:
time: 188 us
  blocking collectives  132 us (70%)
  starting transfers between devices  21.7 us (12%)
  waiting for transfers between devices  14.7 us (8%)
  matrix products  10.4 us (6%)
  local copies, waits for them, and re-layouts  6.82 us (4%)
    psum x1, blocking collectives, per_device(): lax.psum((term_reduce, term_dilated, term_expand), ('lat', 'lon'))  132 us
    ppermute x4, starting transfers between devices, with_halo(): lax.ppermute(head, axis, [((i + 1) % count, i) for i in range(ends)])  12.7 us
    ppermute x4, starting transfers between devices, with_halo(): lax.ppermute(tail, axis, [(i, (i + 1) % count) for i in range(ends)])  9.04 us
    ppermute x4, waiting for transfers between devices, with_halo(): lax.ppermute(head, axis, [((i + 1) % count, i) for i in range(ends)])  7.49 us
    ppermute x4, waiting for transfers between devices, with_halo(): lax.ppermute(tail, axis, [(i, (i + 1) % count) for i in range(ends)])  7.21 us
    unnamed x45, local copies, waits for them, and re-layouts  6.35 us
    dot_general x3, matrix products, pixel_sum(): lax.dot_general(left, right, (((0,), (0,)), ((), ())), preferred_element_...  3.79 us
  transfers between devices with their start and end apart: 8, of which 5 were waited for; matrix products, arithmetic and copies ran while one was open for 2% of the time, Pallas kernels for 0%

commit v1 on v0

--- a/solution.py
+++ b/solution.py
@@ -114,7 +114,7 @@
         jnp.dot(grad_one, w_reduce.T, preferred_element_type=jnp.float32) + grad_full
     ).astype(jnp.bfloat16)
     total_reduce, total_dilated, total_expand = lax.psum(
-        (term_reduce, term_dilated, term_expand), ("lat", "lon")
+        lax.psum((term_reduce, term_dilated, term_expand), "lon"), "lat"
     )
     grad_reduce = total_reduce.astype(jnp.bfloat16)
     grad_dilated = total_dilated.astype(jnp.bfloat16)

time: 188 us -> 283 us (1.51)
  waiting for transfers between devices: 14.7 us -> 130 us
  blocking collectives: 132 us -> 94.3 us
  between operations: 1 us -> 14.4 us
    psum x0 -> x1, waiting for transfers between devices: none -> 116 us  [per_device(): lax.psum((term_reduce, term_dilated, term_expand), 'lon')]
    psum x1, blocking collectives: 132 us -> 94.3 us  [per_device(): lax.psum(lax.psum((term_reduce, term_dilated, term_expand), 'lon'), 'lat')]
  transfers between devices with their start and end apart: 8 -> 9, of which waited for: 5 -> 6; matrix products, arithmetic and copies ran while one was open for 2% -> 2% of each run, Pallas kernels for 0% -> 0%
where the time goes in v1:
time: 283 us; the launch traced here: 280 us
  waiting for transfers between devices  130 us (46%)
  blocking collectives  94.3 us (33%)
  starting transfers between devices  21.8 us (8%)
  between operations  14.4 us (5%)
  matrix products  11.8 us (4%)
  local copies, waits for them, and re-layouts  6.77 us (2%)
    psum x1, waiting for transfers between devices, per_device(): lax.psum((term_reduce, term_dilated, term_expand), 'lon')  116 us
    psum x1, blocking collectives, per_device(): lax.psum(lax.psum((term_reduce, term_dilated, term_expand), 'lon'), 'lat')  94.3 us
    ppermute x4, starting transfers between devices, with_halo(): lax.ppermute(head, axis, [((i + 1) % count, i) for i in range(ends)])  12.7 us
    ppermute x4, starting transfers between devices, with_halo(): lax.ppermute(tail, axis, [(i, (i + 1) % count) for i in range(ends)])  9.03 us
    ppermute x4, waiting for transfers between devices, with_halo(): lax.ppermute(head, axis, [((i + 1) % count, i) for i in range(ends)])  7.49 us
    ppermute x4, waiting for transfers between devices, with_halo(): lax.ppermute(tail, axis, [(i, (i + 1) % count) for i in range(ends)])  7.21 us
    unnamed x45, local copies, waits for them, and re-layouts  6.31 us
  transfers between devices with their start and end apart: 9, of which 6 were waited for; matrix products, arithmetic and copies ran while one was open for 2% of the time, Pallas kernels for 0%

profile of v1, /device:TPU:64, one launch (start us, length us, event | category | flops | bytes accessed | tf_op | source)
XLA Modules:
  0.0 280.4 jit_solution(12945968359879216007)
XLA Ops:
  7.2 1.0 copy-done
  8.2 1.8 multiply_convert_fusion.2
  10.0 3.8 %collective-permute-start = (bf16[4,2,8,256]{3,2,1,0:T(8,128)(2,1)S(1)}, bf16[4,2,8,256]{3,2,1,0:T(8,128)(2,1)S(1)}, u32[]{:S(2)}, u32[]{:S(2)}) collective-permute-start(bf16[4,2,8,256]{3,2,1,0:T(8,128)(2,1)S(1)} %get-tuple-element.48), channel_id=1, source_target_pairs={{0,32},{32,64},{64,96},{96,128},{128,160},{160,192},{192,224},{1,3... | collective-permute-start | bytes 98312 | tf_op jit(solution)/shard_map/ppermute | solution.py:15
  13.9 2.0 collective-permute-start.1
  16.2 1.5 copy.22
  17.7 3.1 %collective-permute-done.1 = bf16[4,2,8,256]{3,2,1,0:T(8,128)(2,1)S(1)} collective-permute-done((bf16[4,2,8,256]{3,2,1,0:T(8,128)(2,1)S(1)}, bf16[4,2,8,256]{3,2,1,0:T(8,128)(2,1)S(1)}, u32[]{:S(2)}, u32[]{:S(2)}) %collective-permute-start.1) | collective-permute-done | bytes 32800 | tf_op jit(solution)/shard_map/ppermute | solution.py:17
  21.0 5.1 %collective-permute-start.3 = (bf16[4,20,2,256]{3,2,1,0:T(2,128)(2,1)S(1)}, bf16[4,20,2,256]{3,2,1,0:T(2,128)(2,1)S(1)}, u32[]{:S(2)}, u32[]{:S(2)}) collective-permute-start(bf16[4,20,2,256]{3,2,1,0:T(2,128)(2,1)S(1)} %get-tuple-element.40), channel_id=1, source_target_pairs={{1,0},{2,1},{3,2},{4,3},{5,4},{6,5},{7,6},{8,7},{9,8},{10,9},{11,1... | collective-permute-start | bytes 245768 | tf_op jit(solution)/shard_map/ppermute | solution.py:17
  26.1 2.1 collective-permute-done.2
  31.1 1.3 fusion
  32.9 2.3 fusion.14
  35.2 5.1 %collective-permute-start.4 = (bf16[4,2,8,256]{3,2,1,0:T(8,128)(2,1)S(1)}, bf16[4,2,8,256]{3,2,1,0:T(8,128)(2,1)S(1)}, u32[]{:S(2)}, u32[]{:S(2)}) collective-permute-start(bf16[4,2,8,256]{3,2,1,0:T(8,128)(2,1)S(1)} %get-tuple-element.44), channel_id=1, source_target_pairs={{0,32},{32,64},{64,96},{96,128},{128,160},{160,192},{192,224},{1,3... | collective-permute-start | bytes 98312 | tf_op jit(solution)/shard_map/ppermute | solution.py:15
  40.4 1.9 collective-permute-start.5
  42.3 1.5 fusion.7
  43.8 2.4 collective-permute-done.5
  46.3 3.7 %collective-permute-start.6 = (bf16[4,20,2,256]{3,2,1,0:T(2,128)(2,1)S(1)}, bf16[4,20,2,256]{3,2,1,0:T(2,128)(2,1)S(1)}, u32[]{:S(2)}, u32[]{:S(2)}) collective-permute-start(bf16[4,20,2,256]{3,2,1,0:T(2,128)(2,1)S(1)} %get-tuple-element.37), channel_id=1, source_target_pairs={{1,0},{2,1},{3,2},{4,3},{5,4},{6,5},{7,6},{8,7},{9,8},{10,9},{11,1... | collective-permute-start | bytes 245768 | tf_op jit(solution)/shard_map/ppermute | solution.py:17
  50.0 2.0 collective-permute-done.6
  52.0 5.1 %collective-permute-done.7 = bf16[4,20,2,256]{3,2,1,0:T(2,128)(2,1)S(1)} collective-permute-done((bf16[4,20,2,256]{3,2,1,0:T(2,128)(2,1)S(1)}, bf16[4,20,2,256]{3,2,1,0:T(2,128)(2,1)S(1)}, u32[]{:S(2)}, u32[]{:S(2)}) %collective-permute-start.7) | collective-permute-done | bytes 81952 | tf_op jit(solution)/shard_map/ppermute | solution.py:15
  58.0 1.0 copy-done.2
  59.1 0.8 fusion.5
  59.9 1.4 convolution_bitcast_fusion
  61.3 1.4 add_convert_fusion
  62.8 115.5 %all-reduce.5.cloned.1.call-done = (f32[1024,256]{0,1:T(8,128)}, f32[2304,256]{1,0:T(8,128)}, f32[256,1024]{1,0:T(8,128)}) async-done(((f32[1024,256]{0,1:T(8,128)}, f32[2304,256]{1,0:T(8,128)}, f32[256,1024]{1,0:T(8,128)}), (f32[1024,256]{0,1:T(8,128)}, f32[2304,256]{1,0:T(8,128)}, f32[256,1024]{1,0:T(8,128)})) %all-reduce.5.cloned.1.call-update) | async-done | bytes 4456464 | tf_op jit(solution)/shard_map/psum | solution.py:117
  178.3 94.3 %all-reduce.6 = (bf16[1024,256]{0,1:T(8,128)(2,1)S(1)}, bf16[2304,256]{1,0:T(8,128)(2,1)}, bf16[256,1024]{1,0:T(8,128)(2,1)}) all-reduce(f32[1024,256]{0,1:T(8,128)} %get-tuple-element.16, f32[2304,256]{1,0:T(8,128)} %get-tuple-element.17, f32[256,1024]{1,0:T(8,128)} %get-tuple-element.18), channel_id=1, replica_groups=mesh['lat'=8,'lon'=32] {'lat'}, use_global_device_ids=true, to_apply=%region_2.3 | all-reduce | flops 1114112 | bytes 6684672 | tf_op jit(solution)/shard_map/psum | solution.py:116
  272.6 1.0 copy.23
  (65 shorter events, 4.8 us)
Async XLA Ops:
  7.2 1.0 copy-start
  7.2 171.1 %all-reduce.5.cloned.1.call-start = ((), (), s32[]{:S(2)}) async-start(), calls=%async_computation | async-start | bytes 8912896 | tf_op jit(solution)/shard_map/psum | solution.py:117
  8.2 7.7 %copy-start.4 = (s32[4,16,8]{1,2,0:T(8,128)S(1)}, s32[4,16,8]{1,2,0:T(8,128)}, u32[]{:S(2)}) copy-start(s32[4,16,8]{1,2,0:T(8,128)} %param.24) | copy-start | bytes 6148
  8.2 7.9 %copy-start.6 = (f32[3]{0:T(128)S(1)}, f32[3]{0:T(128)}, u32[]{:S(2)}) copy-start(f32[3]{0:T(128)} %param.25) | copy-start | bytes 40
  8.2 8.0 %copy-start.1 = (bf16[3,3,256,256]{3,2,1,0:T(8,128)(2,1)S(1)}, bf16[3,3,256,256]{3,2,1,0:T(8,128)(2,1)}, u32[]{:S(2)}) copy-start(bf16[3,3,256,256]{3,2,1,0:T(8,128)(2,1)} %param.17) | copy-start | bytes 3538948
  10.0 7.7 %collective-permute-start = (bf16[4,2,8,256]{3,2,1,0:T(8,128)(2,1)S(1)}, bf16[4,2,8,256]{3,2,1,0:T(8,128)(2,1)S(1)}, u32[]{:S(2)}, u32[]{:S(2)}) collective-permute-start(bf16[4,2,8,256]{3,2,1,0:T(8,128)(2,1)S(1)} %get-tuple-element.48), channel_id=1, source_target_pairs={{0,32},{32,64},{64,96},{96,128},{128,160},{160,192},{192,224},{1,3... | collective-permute-start | bytes 98312 | tf_op jit(solution)/shard_map/ppermute | solution.py:15
  13.9 6.9 %collective-permute-start.1 = (bf16[4,2,8,256]{3,2,1,0:T(8,128)(2,1)S(1)}, bf16[4,2,8,256]{3,2,1,0:T(8,128)(2,1)S(1)}, u32[]{:S(2)}, u32[]{:S(2)}) collective-permute-start(bf16[4,2,8,256]{3,2,1,0:T(8,128)(2,1)S(1)} %get-tuple-element.49), channel_id=1, source_target_pairs={{32,0},{64,32},{96,64},{128,96},{160,128},{192,160},{224,192},{33,... | collective-permute-start | bytes 98312 | tf_op jit(solution)/shard_map/ppermute | solution.py:17
  20.9 7.3 %collective-permute-start.2 = (bf16[4,20,2,256]{3,2,1,0:T(2,128)(2,1)S(1)}, bf16[4,20,2,256]{3,2,1,0:T(2,128)(2,1)S(1)}, u32[]{:S(2)}, u32[]{:S(2)}) collective-permute-start(bf16[4,20,2,256]{3,2,1,0:T(2,128)(2,1)S(1)} %get-tuple-element.41), channel_id=1, source_target_pairs={{0,1},{1,2},{2,3},{3,4},{4,5},{5,6},{6,7},{7,8},{8,9},{9,10},{10,1... | collective-permute-start | bytes 245768 | tf_op jit(solution)/shard_map/ppermute | solution.py:15
  21.0 7.2 %collective-permute-start.3 = (bf16[4,20,2,256]{3,2,1,0:T(2,128)(2,1)S(1)}, bf16[4,20,2,256]{3,2,1,0:T(2,128)(2,1)S(1)}, u32[]{:S(2)}, u32[]{:S(2)}) collective-permute-start(bf16[4,20,2,256]{3,2,1,0:T(2,128)(2,1)S(1)} %get-tuple-element.40), channel_id=1, source_target_pairs={{1,0},{2,1},{3,2},{4,3},{5,4},{6,5},{7,6},{8,7},{9,8},{10,9},{11,1... | collective-permute-start | bytes 245768 | tf_op jit(solution)/shard_map/ppermute | solution.py:17
  28.7 0.7 copy-start.10
  28.8 0.7 copy-start.11
  29.4 1.2 copy-start.3
  29.4 1.2 copy-start.5
  29.5 1.6 copy-start.7
  29.5 1.7 copy-start.8
  29.5 1.7 copy-start.9
  35.2 8.6 %collective-permute-start.4 = (bf16[4,2,8,256]{3,2,1,0:T(8,128)(2,1)S(1)}, bf16[4,2,8,256]{3,2,1,0:T(8,128)(2,1)S(1)}, u32[]{:S(2)}, u32[]{:S(2)}) collective-permute-start(bf16[4,2,8,256]{3,2,1,0:T(8,128)(2,1)S(1)} %get-tuple-element.44), channel_id=1, source_target_pairs={{0,32},{32,64},{64,96},{96,128},{128,160},{160,192},{192,224},{1,3... | collective-permute-start | bytes 98312 | tf_op jit(solution)/shard_map/ppermute | solution.py:15
  40.4 5.8 %collective-permute-start.5 = (bf16[4,2,8,256]{3,2,1,0:T(8,128)(2,1)S(1)}, bf16[4,2,8,256]{3,2,1,0:T(8,128)(2,1)S(1)}, u32[]{:S(2)}, u32[]{:S(2)}) collective-permute-start(bf16[4,2,8,256]{3,2,1,0:T(8,128)(2,1)S(1)} %get-tuple-element.45), channel_id=1, source_target_pairs={{32,0},{64,32},{96,64},{128,96},{160,128},{192,160},{224,192},{33,... | collective-permute-start | bytes 98312 | tf_op jit(solution)/shard_map/ppermute | solution.py:17
  46.3 5.8 %collective-permute-start.6 = (bf16[4,20,2,256]{3,2,1,0:T(2,128)(2,1)S(1)}, bf16[4,20,2,256]{3,2,1,0:T(2,128)(2,1)S(1)}, u32[]{:S(2)}, u32[]{:S(2)}) collective-permute-start(bf16[4,20,2,256]{3,2,1,0:T(2,128)(2,1)S(1)} %get-tuple-element.37), channel_id=1, source_target_pairs={{1,0},{2,1},{3,2},{4,3},{5,4},{6,5},{7,6},{8,7},{9,8},{10,9},{11,1... | collective-permute-start | bytes 245768 | tf_op jit(solution)/shard_map/ppermute | solution.py:17
  50.0 7.2 %collective-permute-start.7 = (bf16[4,20,2,256]{3,2,1,0:T(2,128)(2,1)S(1)}, bf16[4,20,2,256]{3,2,1,0:T(2,128)(2,1)S(1)}, u32[]{:S(2)}, u32[]{:S(2)}) collective-permute-start(bf16[4,20,2,256]{3,2,1,0:T(2,128)(2,1)S(1)} %get-tuple-element.36), channel_id=1, source_target_pairs={{0,1},{1,2},{2,3},{3,4},{4,5},{5,6},{6,7},{7,8},{8,9},{9,10},{10,1... | collective-permute-start | bytes 245768 | tf_op jit(solution)/shard_map/ppermute | solution.py:15
  57.8 1.3 copy-start.2
  57.8 1.3 copy-start.12
Sparse Core Ops, SparseCore 0:
  61.4 116.7 all-reduce.4
